TPU v7x, 32 devices: a whole 2x2x4 slice. The times are simulated.
32 devices in a mesh: groups: 2 (over x), stem: 8 (over z, y), cuts: 2 (over core).
Axes of the slice: x: 2, y: 2, z: 4, core: 2. Of those that a mesh axis runs over, the one named last changes fastest.
Arguments:
- stem: bfloat16 [4, 2, 4096, 1024], P(('groups', 'cuts'), None, 'stem'), parts along dimension 0, may hold values from -6 to 6
- edge_values: int32 [4, 4], P(('groups', 'cuts')), parts along dimension 0, may hold values from 0 to 1
- index_order: int32 [1024], replicated, may hold values from 0 to 1023, each once
- branch_first: bfloat16 [2, 1024, 1024], replicated, may hold values from -0.125 to 0.125
- branch_second: bfloat16 [2, 1024, 1024], replicated, may hold values from -0.125 to 0.125
- branch_third: bfloat16 [2, 1024, 256], replicated, may hold values from -0.125 to 0.125
- edge_table: float32 [16, 2, 256], replicated, may hold values from -6 to 6
- picks: int32 [4096], P('stem'), may hold values from 0 to 511, as said below
Outputs:
- amplitudes: float32 [2, 8192, 256], P(None, ('groups', 'stem')), parts along dimension 1
There are 2 independent parts, one for each index of `groups`. A program takes and returns all parts, laid end to end along the dimension named above; an argument that names none is the same for every part. Nothing has to cross between parts.
Inputs may be any that keep to these rules, and one draw needn't show every extreme that they name: `index_order`: each number of 0 to 1023 once. `picks`: each aligned block of 512 entries names every number of 0 to 511 once.
All inputs are finite; a program needn't handle non-finite values.
Results may differ from a plain program's by a relative error of at most 0.0041.
Values may be sent and summed in bfloat16 or wider, within the bound.
No kernel may reach another device: no remote copies, remote signals or barrier semaphores. Data moves between devices by JAX's collectives and lax.ppermute only.
A program may use at most 64 MiB of HBM per device.

v0:
```python
import jax
import jax.numpy as jnp
from jax import lax
from jax.sharding import PartitionSpec as P


def swapped(value, axis, distance):
    mask = 2**distance
    pairs = [(source, source ^ mask) for source in range(lax.axis_size(axis))]
    return lax.ppermute(value, axis, pairs)


def complex_dot(operand, matrix):
    real = jnp.dot(operand[0], matrix[0], preferred_element_type=jnp.float32) - jnp.dot(
        operand[1], matrix[1], preferred_element_type=jnp.float32
    )
    imag = jnp.dot(operand[0], matrix[1], preferred_element_type=jnp.float32) + jnp.dot(
        operand[1], matrix[0], preferred_element_type=jnp.float32
    )
    return jnp.stack([real, imag])


def on_device(
    stem, edge_values, index_order, branch_first, branch_second, branch_third, edge_table, picks
):
    stem_size = lax.axis_size("stem")
    bit_pos = stem_size.bit_length() - 2
    top_bit = lax.axis_index("stem") // (stem_size // 2) % 2
    is_low = top_bit == 0
    width = branch_first.shape[1]
    half_width = width // 2
    rows_dev = stem.shape[2]
    block_rows = rows_dev // stem_size
    inverse = jnp.zeros_like(index_order).at[index_order].set(jnp.arange(width, dtype=jnp.int32))
    reordered = jnp.take(branch_second, inverse, axis=1)
    powers = 2 ** jnp.arange(edge_values.shape[1], dtype=jnp.int32)
    codes = jnp.arange(edge_table.shape[0], dtype=jnp.int32)
    first = complex_dot(stem[0], branch_first).astype(jnp.bfloat16)
    low_half = first[:, :, :half_width]
    high_half = first[:, :, half_width:]
    outgoing = jnp.where(is_low, high_half, low_half)
    incoming = swapped(outgoing, "stem", bit_pos)
    joined = jnp.where(
        is_low,
        jnp.concatenate([low_half, incoming], axis=2),
        jnp.concatenate([incoming, high_half], axis=2),
    )
    second = complex_dot(joined, reordered).astype(jnp.bfloat16)
    contracted = complex_dot(second, branch_third)
    moved = lax.all_to_all(
        contracted.reshape(2, stem_size, block_rows, contracted.shape[2]),
        "stem",
        split_axis=1,
        concat_axis=1,
        tiled=True,
    )
    third = jnp.take(moved.reshape(2, rows_dev, contracted.shape[2]), picks, axis=1)
    code = jnp.sum(edge_values[0] * powers)
    onehot = (codes == code).astype(jnp.float32)
    factor = jnp.sum(onehot[:, None, None] * edge_table, axis=0)
    real = third[0] * factor[0][None, :] - third[1] * factor[1][None, :]
    imag = third[0] * factor[1][None, :] + third[1] * factor[0][None, :]
    total = jnp.stack([real, imag])
    return lax.psum(total, "cuts")


def solution(mesh):
    return jax.shard_map(
        on_device,
        mesh=mesh,
        in_specs=(
            P(("groups", "cuts"), None, "stem", None),
            P(("groups", "cuts"), None),
            P(),
            P(),
            P(),
            P(),
            P(),
            P("stem"),
        ),
        out_specs=P(None, ("groups", "stem"), None),
        check_vma=False,
    )
```

profile of v0, /device:TPU:0, one launch (start us, length us, event | category | flops | bytes accessed | tf_op | source)
XLA Modules:
  0.0 144.1 jit_solution(4913342444032320021)
XLA Ops:
  6.5 4.6 %fusion.2 = f32[512,1024]{1,0:T(8,128)} fusion(bf16[2,1024,1024]{2,1,0:T(8,128)(2,1)} %param.11, bf16[1,2,512,1024]{3,2,1,0:T(8,128)(2,1)} %param.8), kind=kOutput, calls=%fused_computation.11 | convolution fusion | flops 1073741824 | bytes 5242880 | tf_op jit(solution)/shard_map/dot_general | solution.py:14
  11.2 2.6 %fusion = f32[512,1024]{1,0:T(8,128)} fusion(bf16[2,1024,1024]{2,1,0:T(8,128)(2,1)S(1)} %copy-done.4, bf16[1,2,512,1024]{3,2,1,0:T(8,128)(2,1)S(1)} %copy-done.6), kind=kOutput, calls=%fused_computation.9 | convolution fusion | flops 1073741824 | bytes 5242880 | tf_op jit(solution)/shard_map/dot_general | solution.py:17
  13.8 3.6 %fusion.20 = bf16[1,512,1024]{2,1,0:T(8,128)(2,1)S(1)} fusion(f32[512,1024]{1,0:T(8,128)} %fusion.2, bf16[2,1024,1024]{2,1,0:T(8,128)(2,1)} %param.11, bf16[1,2,512,1024]{3,2,1,0:T(8,128)(2,1)S(1)} %copy-done.6), kind=kOutput, calls=%fused_computation.29 | convolution fusion | flops 1074790400 | bytes 6291456 | tf_op jit(solution)/shard_map/dot_general | solution.py:14
  17.9 1.3 fusion.23
  19.7 4.1 %collective-permute-start = (bf16[2,512,512]{2,1,0:T(8,128)(2,1)S(1)}, bf16[2,512,512]{2,1,0:T(8,128)(2,1)}, u32[]{:S(2)}, u32[]{:S(2)}) collective-permute-start(bf16[2,512,512]{2,1,0:T(8,128)(2,1)S(1)} %get-tuple-element.5), channel_id=1, source_target_pairs={{0,8},{2,10},{4,12},{6,14},{8,0},{10,2},{12,4},{14,6},{1,9},{3,11}... | collective-permute-start | bytes 3145736 | tf_op jit(solution)/shard_map/ppermute | solution.py:10
  23.8 4.5 %scatter_custom_fusion = s32[1024]{0:T(1024)S(1)} fusion(s32[1024]{0:T(1024)S(1)} %compare_select_fusion.1, s32[1024]{0:T(1024)S(1)} %iota.11, s32[]{:T(128)} %constant.69.clone.1), kind=kCustom, calls=%fused_computation.69 | custom fusion | bytes 4100 | tf_op jit(solution)/shard_map/scatter | solution.py:34
  28.3 27.6 %gather_fusion = bf16[1024,2,1024]{2,0,1:T(8,128)(2,1)} fusion(bf16[2,1024,1024]{2,1,0:T(8,128)(2,1)} %param.12, s32[1024]{0:T(1024)S(1)} %fusion.46), kind=kCustom, calls=%fused_computation | custom fusion | bytes 8392704 | tf_op jit(solution)/shard_map/jit(_take)/gather | solution.py:35
  56.0 2.6 %select_bitcast_fusion = bf16[2,1024,1024]{2,1,0:T(8,128)(2,1)S(1)} fusion(bf16[1024,2,1024]{2,0,1:T(8,128)(2,1)} %gather_fusion, pred[1024]{0:T(1024)(128)(4,1)S(1)} %compare_and_fusion), kind=kLoop, calls=%fused_computation.3 | loop fusion | flops 2097152 | bytes 8389632 | tf_op jit(solution)/shard_map/jit(_take)/select_n | solution.py:35
  58.6 10.9 %collective-permute-done = bf16[2,512,512]{2,1,0:T(8,128)(2,1)} collective-permute-done((bf16[2,512,512]{2,1,0:T(8,128)(2,1)S(1)}, bf16[2,512,512]{2,1,0:T(8,128)(2,1)}, u32[]{:S(2)}, u32[]{:S(2)}) %collective-permute-start) | collective-permute-done | bytes 1048608 | tf_op jit(solution)/shard_map/ppermute | solution.py:10
  69.6 2.2 %maximum_select_fusion = bf16[2,512,1024]{2,1,0:T(8,128)(2,1)S(1)} fusion(bf16[2,512,512]{2,1,0:T(8,128)(2,1)} %collective-permute-done, bf16[2,512,512]{2,1,0:T(8,128)(2,1)S(1)} %get-tuple-element.6, bf16[2,512,512]{2,1,0:T(8,128)(2,1)S(1)} %get-tuple-element.7, pred[]{:T(512)S(6)} %eq.15), kind=kLoop, calls=%fused_computation.8 | loop fusion | flops 9437184 | bytes 5242881 | tf_op jit(solution)/shard_map/jit(_where)/select_n | solution.py:43
  71.8 1.3 fusion.8
  73.1 1.3 fusion.11
  74.3 1.3 subtract_convert_fusion
  76.6 1.3 add_convert_fusion
  78.8 1.1 pad_maximum_fusion.1
  79.9 5.8 %all-to-all-start = ((f32[2,8,64,256]{3,2,0,1:T(8,128)}), f32[2,8,64,256]{3,2,0,1:T(8,128)S(1)}, u32[]{:S(2)}, u32[]{:S(2)}) async-start(f32[2,8,64,256]{3,2,0,1:T(8,128)} %pad_maximum_fusion.1), calls=%async_computation | async-start | bytes 2097152 | tf_op jit(solution)/shard_map/all_to_all | solution.py:50
  85.7 0.6 fusion.52
  86.3 0.6 compare_convert_fusion
  87.1 24.5 %all-to-all-done = f32[2,8,64,256]{3,2,0,1:T(8,128)S(1)} async-done(((f32[2,8,64,256]{3,2,0,1:T(8,128)}), f32[2,8,64,256]{3,2,0,1:T(8,128)S(1)}, u32[]{:S(2)}, u32[]{:S(2)}) %all-to-all-start) | async-done | bytes 1048608 | tf_op jit(solution)/shard_map/all_to_all | solution.py:50
  111.6 0.8 copy.17
  112.4 2.6 %gather_fusion.1 = f32[512,2,256]{2,1,0:T(2,128)S(1)} fusion(f32[2,512,256]{2,0,1:T(2,128)S(1)} %bitcast.83, s32[1024]{0:T(1024)S(1)} %pad_clamp_fusion), kind=kCustom, calls=%fused_computation.1 | custom fusion | bytes 2099200 | tf_op jit(solution)/shard_map/jit(_take)/gather | solution.py:57
  115.3 1.0 pad_maximum_fusion.2
  116.3 18.6 %all-reduce.2.cloned.1.call-done = f32[2,512,256]{2,1,0:T(8,128)} async-done(((f32[2,512,256]{2,1,0:T(8,128)}), f32[2,512,256]{2,1,0:T(8,128)}) %all-reduce.2.cloned.1.call-update) | async-done | bytes 1048592 | tf_op jit(solution)/shard_map/psum | solution.py:64
  135.0 2.3 %copy.23 = f32[2,512,256]{2,1,0:T(8,128)} copy(f32[2,512,256]{2,1,0:T(8,128)} %all-reduce.2.cloned.1.call-done) | data formatting | bytes 2097152
  (36 shorter events, 3.3 us)
Async XLA Ops:
  6.5 4.6 %copy-start.4 = (bf16[2,1024,1024]{2,1,0:T(8,128)(2,1)S(1)}, bf16[2,1024,1024]{2,1,0:T(8,128)(2,1)}, u32[]{:S(2)}) copy-start(bf16[2,1024,1024]{2,1,0:T(8,128)(2,1)} %param.11) | copy-start | bytes 12582916
  6.5 4.6 %copy-start.6 = (bf16[1,2,512,1024]{3,2,1,0:T(8,128)(2,1)S(1)}, bf16[1,2,512,1024]{3,2,1,0:T(8,128)(2,1)}, u32[]{:S(2)}) copy-start(bf16[1,2,512,1024]{3,2,1,0:T(8,128)(2,1)} %param.8) | copy-start | bytes 6291460
  13.8 3.6 %copy-start.5 = (bf16[2,1024,1024]{2,1,0:T(8,128)(2,1)S(1)}, bf16[2,1024,1024]{2,1,0:T(8,128)(2,1)}, u32[]{:S(2)}) copy-start(bf16[2,1024,1024]{2,1,0:T(8,128)(2,1)} %param.11) | copy-start | bytes 12582916
  13.8 4.1 %copy-start.8 = (f32[512,1024]{1,0:T(8,128)S(1)}, f32[512,1024]{1,0:T(8,128)}, u32[]{:S(2)}) copy-start(f32[512,1024]{1,0:T(8,128)} %fusion) | copy-start | bytes 6291460
  19.2 4.6 %copy-start.3 = (s32[1024]{0:T(1024)S(1)}, s32[1024]{0:T(1024)}, u32[]{:S(2)}) copy-start(s32[1024]{0:T(1024)} %param.10) | copy-start | bytes 12292
  19.7 49.9 %collective-permute-start = (bf16[2,512,512]{2,1,0:T(8,128)(2,1)S(1)}, bf16[2,512,512]{2,1,0:T(8,128)(2,1)}, u32[]{:S(2)}, u32[]{:S(2)}) collective-permute-start(bf16[2,512,512]{2,1,0:T(8,128)(2,1)S(1)} %get-tuple-element.5), channel_id=1, source_target_pairs={{0,8},{2,10},{4,12},{6,14},{8,0},{10,2},{12,4},{14,6},{1,9},{3,11}... | collective-permute-start | bytes 3145736 | tf_op jit(solution)/shard_map/ppermute | solution.py:10
  74.3 1.3 copy-start
  78.8 6.9 %copy-start.7 = (s32[1,4]{1,0:T(1,128)S(1)}, s32[1,4]{1,0:T(1,128)}, u32[]{:S(2)}) copy-start(s32[1,4]{1,0:T(1,128)} %param.9) | copy-start | bytes 52
  78.8 8.1 %copy-start.2 = (s32[512]{0:T(512)S(1)}, s32[512]{0:T(512)}, u32[]{:S(2)}) copy-start(s32[512]{0:T(512)} %param.15) | copy-start | bytes 6148
  78.8 8.1 %copy-start.1 = (f32[16,2,256]{2,1,0:T(2,128)S(1)}, f32[16,2,256]{2,1,0:T(2,128)}, u32[]{:S(2)}) copy-start(f32[16,2,256]{2,1,0:T(2,128)} %param.14) | copy-start | bytes 98308
  79.9 31.7 %all-to-all-start = ((f32[2,8,64,256]{3,2,0,1:T(8,128)}), f32[2,8,64,256]{3,2,0,1:T(8,128)S(1)}, u32[]{:S(2)}, u32[]{:S(2)}) async-start(f32[2,8,64,256]{3,2,0,1:T(8,128)} %pad_maximum_fusion.1), calls=%async_computation | async-start | bytes 2097152 | tf_op jit(solution)/shard_map/all_to_all | solution.py:50
  85.7 49.3 %all-reduce.2.cloned.1.call-start = ((), (), s32[]{:S(2)}) async-start(), calls=%async_computation.1 | async-start | bytes 2097152 | tf_op jit(solution)/shard_map/psum | solution.py:64
Sparse Core Ops, SparseCore 0:
  116.5 18.4 all-reduce.1
where the time goes:
time: 145 us; the launch traced here: 144 us
  waiting for transfers between devices  54.1 us (37%)
  local copies, waits for them, and re-layouts  38.3 us (26%)
  matrix products  19.1 us (13%)
  between operations  13.7 us (9%)
  starting transfers between devices  9.93 us (7%)
  other arithmetic  9.01 us (6%)
    gather x1, local copies, waits for them, and re-layouts, on_device(): reordered = jnp.take(branch_second, inverse, axis=1)  27.6 us
    all_to_all x1, waiting for transfers between devices, on_device(): lax.all_to_all(contracted.reshape(2, stem_size, block_rows, contracted.sh...  24.5 us
    psum x1, waiting for transfers between devices, on_device(): return lax.psum(total, 'cuts')  18.6 us
    ppermute x1, waiting for transfers between devices, swapped(): return lax.ppermute(value, axis, pairs)  10.9 us
    dot_general x3, matrix products, complex_dot(): jnp.dot(operand[1], matrix[1], preferred_element_type=jnp.float32)  6.33 us
    all_to_all x1, starting transfers between devices, on_device(): lax.all_to_all(contracted.reshape(2, stem_size, block_rows, contracted.sh...  5.77 us
    dot_general x3, matrix products, complex_dot(): jnp.dot(operand[0], matrix[0], preferred_element_type=jnp.float32)  5.36 us
    scatter x1, local copies, waits for them, and re-layouts, on_device(): jnp.zeros_like(index_order).at[index_order]  4.49 us
  transfers between devices with their start and end apart: 3, of which 3 were waited for; matrix products, arithmetic and copies ran while one was open for 25% of the time, Pallas kernels for 0%

commit v1 on v0

--- a/solution.py
+++ b/solution.py
@@ -47,13 +47,20 @@
     )
     second = complex_dot(joined, reordered).astype(jnp.bfloat16)
     contracted = complex_dot(second, branch_third)
-    moved = lax.all_to_all(
-        contracted.reshape(2, stem_size, block_rows, contracted.shape[2]),
-        "stem",
-        split_axis=1,
-        concat_axis=1,
-        tiled=True,
-    )
+    shard = contracted.reshape(2, stem_size, block_rows, contracted.shape[2])
+    ways, here = (lax.axis_size("stem"), lax.axis_index("stem"))
+    width_2 = shard.shape[1] // ways
+    dims = list(shard.shape)
+    dims[1] = width_2
+    height = dims[1]
+    dims[1] = height * ways
+    full = jnp.zeros(dims, shard.dtype)
+    for mask_2 in range(ways):
+        part = lax.dynamic_slice_in_dim(shard, (here ^ mask_2) * width_2, width_2, axis=1)
+        if mask_2:
+            part = lax.ppermute(part, "stem", [(d, d ^ mask_2) for d in range(ways)])
+        full = lax.dynamic_update_slice_in_dim(full, part, (here ^ mask_2) * height, axis=1)
+    moved = full
     third = jnp.take(moved.reshape(2, rows_dev, contracted.shape[2]), picks, axis=1)
     code = jnp.sum(edge_values[0] * powers)
     onehot = (codes == code).astype(jnp.float32)

time: 145 us -> 138 us (0.952)
  waiting for transfers between devices: 54.1 us -> 39.4 us
  starting transfers between devices: 9.93 us -> 18 us
    all_to_all x1 -> x0, waiting for transfers between devices: 24.5 us -> none  [on_device(): lax.all_to_all(contracted.reshape(2, stem_size, block_rows, contracted.sh...]
    ppermute x0 -> x7, starting transfers between devices: none -> 13.9 us  [on_device(): part = lax.ppermute(part, 'stem', [(d, d ^ mask_2) for d in range(ways)])]
    ppermute x0 -> x7, waiting for transfers between devices: none -> 7.35 us  [on_device(): part = lax.ppermute(part, 'stem', [(d, d ^ mask_2) for d in range(ways)])]
    all_to_all x1 -> x0, starting transfers between devices: 5.77 us -> none  [on_device(): lax.all_to_all(contracted.reshape(2, stem_size, block_rows, contracted.sh...]
    psum x1, waiting for transfers between devices: 18.6 us -> 22.8 us  [on_device(): return lax.psum(total, 'cuts')]
    ppermute x1, waiting for transfers between devices: 10.9 us -> 9.26 us  [swapped(): return lax.ppermute(value, axis, pairs)]
  transfers between devices with their start and end apart: 3 -> 9, of which waited for: 3 -> 6; matrix products, arithmetic and copies ran while one was open for 25% -> 27% of each run, Pallas kernels for 0% -> 0%
where the time goes in v1:
time: 138 us; the launch traced here: 137 us
  waiting for transfers between devices  39.4 us (29%)
  local copies, waits for them, and re-layouts  38.8 us (28%)
  matrix products  19.1 us (14%)
  starting transfers between devices  18 us (13%)
  between operations  13.7 us (10%)
  other arithmetic  8.01 us (6%)
    gather x1, local copies, waits for them, and re-layouts, on_device(): reordered = jnp.take(branch_second, inverse, axis=1)  27.8 us
    psum x1, waiting for transfers between devices, on_device(): return lax.psum(total, 'cuts')  22.8 us
    ppermute x7, starting transfers between devices, on_device(): part = lax.ppermute(part, 'stem', [(d, d ^ mask_2) for d in range(ways)])  13.9 us
    ppermute x1, waiting for transfers between devices, swapped(): return lax.ppermute(value, axis, pairs)  9.26 us
    ppermute x7, waiting for transfers between devices, on_device(): part = lax.ppermute(part, 'stem', [(d, d ^ mask_2) for d in range(ways)])  7.35 us
    dot_general x3, matrix products, complex_dot(): jnp.dot(operand[1], matrix[1], preferred_element_type=jnp.float32)  6.35 us
    dot_general x3, matrix products, complex_dot(): jnp.dot(operand[0], matrix[0], preferred_element_type=jnp.float32)  5.39 us
    scatter x1, local copies, waits for them, and re-layouts, on_device(): jnp.zeros_like(index_order).at[index_order]  4.49 us
  transfers between devices with their start and end apart: 9, of which 6 were waited for; matrix products, arithmetic and copies ran while one was open for 27% of the time, Pallas kernels for 0%

profile of v1, /device:TPU:0, one launch (start us, length us, event | category | flops | bytes accessed | tf_op | source)
XLA Modules:
  0.0 137.1 jit_solution(10652034518276904812)
XLA Ops:
  6.5 4.6 %fusion.2 = f32[512,1024]{1,0:T(8,128)} fusion(bf16[2,1024,1024]{2,1,0:T(8,128)(2,1)} %param.11, bf16[1,2,512,1024]{3,2,1,0:T(8,128)(2,1)} %param.8), kind=kOutput, calls=%fused_computation.27 | convolution fusion | flops 1073741824 | bytes 5242880 | tf_op jit(solution)/shard_map/dot_general | solution.py:14
  11.2 2.6 %fusion = f32[512,1024]{1,0:T(8,128)} fusion(bf16[2,1024,1024]{2,1,0:T(8,128)(2,1)S(1)} %copy-done.4, bf16[1,2,512,1024]{3,2,1,0:T(8,128)(2,1)S(1)} %copy-done.6), kind=kOutput, calls=%fused_computation.25 | convolution fusion | flops 1073741824 | bytes 5242880 | tf_op jit(solution)/shard_map/dot_general | solution.py:17
  13.8 3.6 %fusion.20 = bf16[1,512,1024]{2,1,0:T(8,128)(2,1)S(1)} fusion(f32[512,1024]{1,0:T(8,128)} %fusion.2, bf16[2,1024,1024]{2,1,0:T(8,128)(2,1)} %param.11, bf16[1,2,512,1024]{3,2,1,0:T(8,128)(2,1)S(1)} %copy-done.6), kind=kOutput, calls=%fused_computation.45 | convolution fusion | flops 1074790400 | bytes 6291456 | tf_op jit(solution)/shard_map/dot_general | solution.py:14
  17.9 1.3 fusion.23
  19.7 4.1 %collective-permute-start = (bf16[2,512,512]{2,1,0:T(8,128)(2,1)S(1)}, bf16[2,512,512]{2,1,0:T(8,128)(2,1)}, u32[]{:S(2)}, u32[]{:S(2)}) collective-permute-start(bf16[2,512,512]{2,1,0:T(8,128)(2,1)S(1)} %get-tuple-element.5), channel_id=1, source_target_pairs={{0,8},{2,10},{4,12},{6,14},{8,0},{10,2},{12,4},{14,6},{1,9},{3,11}... | collective-permute-start | bytes 3145736 | tf_op jit(solution)/shard_map/ppermute | solution.py:10
  23.9 4.5 %scatter_custom_fusion = s32[1024]{0:T(1024)S(1)} fusion(s32[1024]{0:T(1024)S(1)} %compare_select_fusion.1, s32[1024]{0:T(1024)S(1)} %iota.11, s32[]{:T(128)} %constant.46.clone.1), kind=kCustom, calls=%fused_computation.100 | custom fusion | bytes 4100 | tf_op jit(solution)/shard_map/scatter | solution.py:34
  29.7 27.8 %gather_fusion = bf16[1024,2,1024]{2,0,1:T(8,128)(2,1)} fusion(bf16[2,1024,1024]{2,1,0:T(8,128)(2,1)} %param.12, s32[1024]{0:T(1024)S(1)} %fusion.54), kind=kCustom, calls=%fused_computation | custom fusion | bytes 8392704 | tf_op jit(solution)/shard_map/jit(_take)/gather | solution.py:35
  57.7 2.6 %select_bitcast_fusion = bf16[2,1024,1024]{2,1,0:T(8,128)(2,1)S(1)} fusion(bf16[1024,2,1024]{2,0,1:T(8,128)(2,1)} %gather_fusion, pred[1024]{0:T(1024)(128)(4,1)S(1)} %compare_and_fusion), kind=kLoop, calls=%fused_computation.3 | loop fusion | flops 2097152 | bytes 8389632 | tf_op jit(solution)/shard_map/jit(_take)/select_n | solution.py:35
  60.3 9.3 %collective-permute-done = bf16[2,512,512]{2,1,0:T(8,128)(2,1)} collective-permute-done((bf16[2,512,512]{2,1,0:T(8,128)(2,1)S(1)}, bf16[2,512,512]{2,1,0:T(8,128)(2,1)}, u32[]{:S(2)}, u32[]{:S(2)}) %collective-permute-start) | collective-permute-done | bytes 1048608 | tf_op jit(solution)/shard_map/ppermute | solution.py:10
  69.6 2.1 %maximum_select_fusion = bf16[2,512,1024]{2,1,0:T(8,128)(2,1)S(1)} fusion(bf16[2,512,512]{2,1,0:T(8,128)(2,1)} %collective-permute-done, bf16[2,512,512]{2,1,0:T(8,128)(2,1)S(1)} %get-tuple-element.6, bf16[2,512,512]{2,1,0:T(8,128)(2,1)S(1)} %get-tuple-element.7, pred[]{:T(512)S(6)} %eq.15), kind=kLoop, calls=%fused_computation.24 | loop fusion | flops 9437184 | bytes 5242881 | tf_op jit(solution)/shard_map/jit(_where)/select_n | solution.py:43
  71.7 1.3 fusion.8
  73.0 1.3 fusion.11
  74.2 1.3 subtract_convert_fusion
  76.5 1.3 add_convert_fusion
  79.3 1.2 collective-permute-start.1
  80.5 4.0 %collective-permute-start.2 = (f32[2,1,64,256]{3,2,1,0:T(8,128)S(1)}, f32[2,1,64,256]{3,2,1,0:T(8,128)S(1)}, u32[]{:S(2)}, u32[]{:S(2)}) collective-permute-start(f32[2,1,64,256]{3,2,1,0:T(8,128)S(1)} %get-tuple-element.13), channel_id=1, source_target_pairs={{0,4},{2,6},{4,0},{6,2},{8,12},{10,14},{12,8},{14,10},{1,5},{3,7},... | collective-permute-start | bytes 393224 | tf_op jit(solution)/shard_map/ppermute | solution.py:61
  86.7 4.1 %collective-permute-start.6 = (f32[2,1,64,256]{3,2,1,0:T(8,128)S(1)}, f32[2,1,64,256]{3,2,1,0:T(8,128)S(1)}, u32[]{:S(2)}, u32[]{:S(2)}) collective-permute-start(f32[2,1,64,256]{3,2,1,0:T(8,128)S(1)} %get-tuple-element.16), channel_id=1, source_target_pairs={{0,12},{2,14},{4,8},{6,10},{8,4},{10,6},{12,0},{14,2},{1,13},{3,15... | collective-permute-start | bytes 393224 | tf_op jit(solution)/shard_map/ppermute | solution.py:61
  90.9 2.1 %collective-permute-done.2 = f32[2,1,64,256]{3,2,1,0:T(8,128)S(1)} collective-permute-done((f32[2,1,64,256]{3,2,1,0:T(8,128)S(1)}, f32[2,1,64,256]{3,2,1,0:T(8,128)S(1)}, u32[]{:S(2)}, u32[]{:S(2)}) %collective-permute-start.2) | collective-permute-done | bytes 131104 | tf_op jit(solution)/shard_map/ppermute | solution.py:61
  93.0 2.3 %collective-permute-start.7 = (f32[2,1,64,256]{3,2,1,0:T(8,128)S(1)}, f32[2,1,64,256]{3,2,1,0:T(8,128)S(1)}, u32[]{:S(2)}, u32[]{:S(2)}) collective-permute-start(f32[2,1,64,256]{3,2,1,0:T(8,128)S(1)} %get-tuple-element.10), channel_id=1, source_target_pairs={{0,14},{2,12},{4,10},{6,8},{8,6},{10,4},{12,2},{14,0},{1,15},{3,13... | collective-permute-start | bytes 393224 | tf_op jit(solution)/shard_map/ppermute | solution.py:61
  96.5 2.1 %collective-permute-done.6 = f32[2,1,64,256]{3,2,1,0:T(8,128)S(1)} collective-permute-done((f32[2,1,64,256]{3,2,1,0:T(8,128)S(1)}, f32[2,1,64,256]{3,2,1,0:T(8,128)S(1)}, u32[]{:S(2)}, u32[]{:S(2)}) %collective-permute-start.6) | collective-permute-done | bytes 131104 | tf_op jit(solution)/shard_map/ppermute | solution.py:61
  98.6 2.5 %collective-permute-done.7 = f32[2,1,64,256]{3,2,1,0:T(8,128)S(1)} collective-permute-done((f32[2,1,64,256]{3,2,1,0:T(8,128)S(1)}, f32[2,1,64,256]{3,2,1,0:T(8,128)S(1)}, u32[]{:S(2)}, u32[]{:S(2)}) %collective-permute-start.7) | collective-permute-done | bytes 131104 | tf_op jit(solution)/shard_map/ppermute | solution.py:61
  101.2 2.6 %gather_fusion.1 = f32[512,2,256]{2,1,0:T(2,128)S(1)} fusion(f32[2,512,256]{2,0,1:T(2,128)S(1)} %bitcast.83, s32[1024]{0:T(1024)S(1)} %pad_clamp_fusion), kind=kCustom, calls=%fused_computation.1 | custom fusion | bytes 2099200 | tf_op jit(solution)/shard_map/jit(_take)/gather | solution.py:64
  105.2 22.8 %all-reduce.2.cloned.1.call-done = f32[2,512,256]{2,1,0:T(8,128)} async-done(((f32[2,512,256]{2,1,0:T(8,128)}), f32[2,512,256]{2,1,0:T(8,128)}) %all-reduce.2.cloned.1.call-update) | async-done | bytes 1048592 | tf_op jit(solution)/shard_map/psum | solution.py:71
  128.0 2.3 %copy.47 = f32[2,512,256]{2,1,0:T(8,128)} copy(f32[2,512,256]{2,1,0:T(8,128)} %all-reduce.2.cloned.1.call-done) | data formatting | bytes 2097152
  (57 shorter events, 9.9 us)
Async XLA Ops:
  6.5 121.5 %all-reduce.2.cloned.1.call-start = ((), (), s32[]{:S(2)}) async-start(), calls=%async_computation | async-start | bytes 2097152 | tf_op jit(solution)/shard_map/psum | solution.py:71
  6.5 4.6 %copy-start.4 = (bf16[2,1024,1024]{2,1,0:T(8,128)(2,1)S(1)}, bf16[2,1024,1024]{2,1,0:T(8,128)(2,1)}, u32[]{:S(2)}) copy-start(bf16[2,1024,1024]{2,1,0:T(8,128)(2,1)} %param.11) | copy-start | bytes 12582916
  6.5 4.6 %copy-start.6 = (bf16[1,2,512,1024]{3,2,1,0:T(8,128)(2,1)S(1)}, bf16[1,2,512,1024]{3,2,1,0:T(8,128)(2,1)}, u32[]{:S(2)}) copy-start(bf16[1,2,512,1024]{3,2,1,0:T(8,128)(2,1)} %param.8) | copy-start | bytes 6291460
  13.8 3.7 %copy-start.5 = (bf16[2,1024,1024]{2,1,0:T(8,128)(2,1)S(1)}, bf16[2,1024,1024]{2,1,0:T(8,128)(2,1)}, u32[]{:S(2)}) copy-start(bf16[2,1024,1024]{2,1,0:T(8,128)(2,1)} %param.11) | copy-start | bytes 12582916
  13.8 4.1 %copy-start.8 = (f32[512,1024]{1,0:T(8,128)S(1)}, f32[512,1024]{1,0:T(8,128)}, u32[]{:S(2)}) copy-start(f32[512,1024]{1,0:T(8,128)} %fusion) | copy-start | bytes 6291460
  19.2 4.6 %copy-start.2 = (s32[512]{0:T(512)S(1)}, s32[512]{0:T(512)}, u32[]{:S(2)}) copy-start(s32[512]{0:T(512)} %param.15) | copy-start | bytes 6148
  19.2 4.6 %copy-start.3 = (s32[1024]{0:T(1024)S(1)}, s32[1024]{0:T(1024)}, u32[]{:S(2)}) copy-start(s32[1024]{0:T(1024)} %param.10) | copy-start | bytes 12292
  19.2 9.2 %copy-start.7 = (s32[1,4]{1,0:T(1,128)S(1)}, s32[1,4]{1,0:T(1,128)}, u32[]{:S(2)}) copy-start(s32[1,4]{1,0:T(1,128)} %param.9) | copy-start | bytes 52
  19.7 49.9 %collective-permute-start = (bf16[2,512,512]{2,1,0:T(8,128)(2,1)S(1)}, bf16[2,512,512]{2,1,0:T(8,128)(2,1)}, u32[]{:S(2)}, u32[]{:S(2)}) collective-permute-start(bf16[2,512,512]{2,1,0:T(8,128)(2,1)S(1)} %get-tuple-element.5), channel_id=1, source_target_pairs={{0,8},{2,10},{4,12},{6,14},{8,0},{10,2},{12,4},{14,6},{1,9},{3,11}... | collective-permute-start | bytes 3145736 | tf_op jit(solution)/shard_map/ppermute | solution.py:10
  29.7 27.8 %copy-start.1 = (f32[16,2,256]{2,1,0:T(2,128)S(1)}, f32[16,2,256]{2,1,0:T(2,128)}, u32[]{:S(2)}) copy-start(f32[16,2,256]{2,1,0:T(2,128)} %param.14) | copy-start | bytes 98308
  74.2 1.3 copy-start
  78.7 17.6 %collective-permute-start.5 = (f32[2,1,64,256]{3,2,1,0:T(8,128)S(1)}, f32[2,1,64,256]{3,2,1,0:T(8,128)S(1)}, u32[]{:S(2)}, u32[]{:S(2)}) collective-permute-start(f32[2,1,64,256]{3,2,1,0:T(8,128)S(1)} %get-tuple-element.17), channel_id=1, source_target_pairs={{0,10},{2,8},{4,14},{6,12},{8,2},{10,0},{12,6},{14,4},{1,11},{3,9}... | collective-permute-start | bytes 393224 | tf_op jit(solution)/shard_map/ppermute | solution.py:61
  79.3 7.4 %collective-permute-start.1 = (f32[2,1,64,256]{3,2,1,0:T(8,128)S(1)}, f32[2,1,64,256]{3,2,1,0:T(8,128)S(1)}, u32[]{:S(2)}, u32[]{:S(2)}) collective-permute-start(f32[2,1,64,256]{3,2,1,0:T(8,128)S(1)} %get-tuple-element.12), channel_id=1, source_target_pairs={{0,2},{2,0},{4,6},{6,4},{8,10},{10,8},{12,14},{14,12},{1,3},{3,1},... | collective-permute-start | bytes 393224 | tf_op jit(solution)/shard_map/ppermute | solution.py:61
  80.5 12.5 %collective-permute-start.2 = (f32[2,1,64,256]{3,2,1,0:T(8,128)S(1)}, f32[2,1,64,256]{3,2,1,0:T(8,128)S(1)}, u32[]{:S(2)}, u32[]{:S(2)}) collective-permute-start(f32[2,1,64,256]{3,2,1,0:T(8,128)S(1)} %get-tuple-element.13), channel_id=1, source_target_pairs={{0,4},{2,6},{4,0},{6,2},{8,12},{10,14},{12,8},{14,10},{1,5},{3,7},... | collective-permute-start | bytes 393224 | tf_op jit(solution)/shard_map/ppermute | solution.py:61
  84.5 11.6 %collective-permute-start.3 = (f32[2,1,64,256]{3,2,1,0:T(8,128)S(1)}, f32[2,1,64,256]{3,2,1,0:T(8,128)S(1)}, u32[]{:S(2)}, u32[]{:S(2)}) collective-permute-start(f32[2,1,64,256]{3,2,1,0:T(8,128)S(1)} %get-tuple-element.14), channel_id=1, source_target_pairs={{0,6},{2,4},{4,2},{6,0},{8,14},{10,12},{12,10},{14,8},{1,7},{3,5},... | collective-permute-start | bytes 393224 | tf_op jit(solution)/shard_map/ppermute | solution.py:61
  85.4 10.8 %collective-permute-start.4 = (f32[2,1,64,256]{3,2,1,0:T(8,128)S(1)}, f32[2,1,64,256]{3,2,1,0:T(8,128)S(1)}, u32[]{:S(2)}, u32[]{:S(2)}) collective-permute-start(f32[2,1,64,256]{3,2,1,0:T(8,128)S(1)} %get-tuple-element.15), channel_id=1, source_target_pairs={{0,8},{2,10},{4,12},{6,14},{8,0},{10,2},{12,4},{14,6},{1,9},{3,11}... | collective-permute-start | bytes 393224 | tf_op jit(solution)/shard_map/ppermute | solution.py:61
  86.7 11.8 %collective-permute-start.6 = (f32[2,1,64,256]{3,2,1,0:T(8,128)S(1)}, f32[2,1,64,256]{3,2,1,0:T(8,128)S(1)}, u32[]{:S(2)}, u32[]{:S(2)}) collective-permute-start(f32[2,1,64,256]{3,2,1,0:T(8,128)S(1)} %get-tuple-element.16), channel_id=1, source_target_pairs={{0,12},{2,14},{4,8},{6,10},{8,4},{10,6},{12,0},{14,2},{1,13},{3,15... | collective-permute-start | bytes 393224 | tf_op jit(solution)/shard_map/ppermute | solution.py:61
  93.0 8.2 %collective-permute-start.7 = (f32[2,1,64,256]{3,2,1,0:T(8,128)S(1)}, f32[2,1,64,256]{3,2,1,0:T(8,128)S(1)}, u32[]{:S(2)}, u32[]{:S(2)}) collective-permute-start(f32[2,1,64,256]{3,2,1,0:T(8,128)S(1)} %get-tuple-element.10), channel_id=1, source_target_pairs={{0,14},{2,12},{4,10},{6,8},{8,6},{10,4},{12,2},{14,0},{1,15},{3,13... | collective-permute-start | bytes 393224 | tf_op jit(solution)/shard_map/ppermute | solution.py:61
Sparse Core Ops, SparseCore 0:
  105.3 22.6 all-reduce.1
